TPU v7x, 32 devices: a whole 2x2x4 slice. The times are simulated.
32 devices in a mesh: gx: 4 (over x, core), gy: 8 (over z, y).
Axes of the slice: x: 2, y: 2, z: 4, core: 2. Of those that a mesh axis runs over, the one named last changes fastest.
Arguments:
- patches: bfloat16 [4096, 1664], P('gy', 'gx'), may hold values from -6 to 6
- segment_ids: int32 [4096], P('gy'), may hold values from 0 to 31, as said below
- image_requests: int32 [32], replicated, may hold values from 0 to 7
- merge_index: int32 [1024, 4], P('gy'), may hold values from 0 to 4095, as said below
- qkv_weight: bfloat16 [1664, 3, 1664], P('gy', None, 'gx'), may hold values from -128 to 128
- out_weight: bfloat16 [1664, 1664], P('gx', 'gy'), may hold values from -0.15625 to 0.15625
- up_weight: bfloat16 [1664, 8192], P('gy', 'gx'), may hold values from -0.15625 to 0.15625
- down_weight: bfloat16 [8192, 1664], P('gx', 'gy'), may hold values from -0.0625 to 0.0625
- merge_weight: bfloat16 [6656, 4096], P('gy', 'gx'), may hold values from -0.078125 to 0.078125
Outputs:
- merged: bfloat16 [1024, 4096], P('gy', 'gx')
- request_norms: float32 [8], replicated
- top_logit: float32 [], replicated
Inputs may be any that keep to these rules, and one draw needn't show every extreme that they name: `segment_ids`: segment ids never fall along the tokens; the 512 tokens of block b (tokens b * 512 onward) hold exactly the images b * 4 to (b + 1) * 4 - 1, each a multiple of 4 tokens long. `merge_index`: every token stands in exactly one merged row; the four tokens of merged row m belong to one image, in the block of 512 tokens that holds token 4 * m.
All inputs are finite; a program needn't handle non-finite values.
Results may differ from a plain program's by a relative error of at most 0.011.
Values may be sent and summed in bfloat16 or wider, within the bound.
A program may use at most 128 MiB of HBM per device.

v0:
```python
import math
import jax
import jax.numpy as jnp
from jax import lax
from jax.sharding import PartitionSpec as P

HEAD = 104
IMG_GRP = 4


def layer_norm(values):
    center = jnp.mean(values, axis=-1, keepdims=True)
    square = jnp.mean(values * values, axis=-1, keepdims=True)
    return (values - center) * lax.rsqrt(square - center * center + 1e-06)


def add_columns(left, piece):
    flat = piece.reshape(piece.shape[0], -1)
    return jnp.dot(left, flat, preferred_element_type=jnp.float32)


def finish_sum(head_partial, stream_full, feat_share):
    own_index = lax.axis_index("gx")
    summed = lax.psum(head_partial, "gx")
    new_full = (stream_full.astype(jnp.float32) + summed).astype(jnp.bfloat16)
    new_share = lax.dynamic_slice_in_dim(new_full, own_index * feat_share, feat_share, 1)
    return (new_full, new_share)


def per_device(
    patches,
    segment_ids,
    image_requests,
    merge_index,
    qkv_weight,
    out_weight,
    up_weight,
    down_weight,
    merge_weight,
):
    tok_rows = patches.shape[0]
    feat_share = patches.shape[1]
    group_index = lax.axis_index("gy")
    stream_full = lax.all_gather(patches, "gx", axis=1, tiled=True)
    normed = layer_norm(stream_full.astype(jnp.float32)).astype(jnp.bfloat16)
    head_share = qkv_weight.shape[2]
    local_heads = head_share // HEAD
    projected = add_columns(normed, lax.all_gather(qkv_weight, "gy", axis=0, tiled=True))
    projected = projected.astype(jnp.bfloat16).reshape(tok_rows, 3, local_heads, HEAD)
    scores = jnp.einsum(
        "qhe,khe->hqk", projected[:, 0], projected[:, 1], preferred_element_type=jnp.float32
    ) / math.sqrt(HEAD)
    allowed = segment_ids[:, None] == segment_ids[None, :]
    scores = jnp.where(allowed[None], scores, -1e30)
    probs = jax.nn.softmax(scores, axis=-1).astype(jnp.bfloat16)
    mixed = jnp.einsum("hqk,khe->qhe", probs, projected[:, 2], preferred_element_type=jnp.float32)
    mixed = mixed.astype(jnp.bfloat16).reshape(tok_rows, head_share)
    head_partial = jnp.dot(
        mixed,
        lax.all_gather(out_weight, "gy", axis=1, tiled=True),
        preferred_element_type=jnp.float32,
    )
    stream_full, stream_share = finish_sum(head_partial, stream_full, feat_share)
    normed_two = layer_norm(stream_full.astype(jnp.float32)).astype(jnp.bfloat16)
    hidden = add_columns(normed_two, lax.all_gather(up_weight, "gy", axis=0, tiled=True))
    hidden = jax.nn.gelu(hidden, approximate=False).astype(jnp.bfloat16)
    unit_partial = jnp.dot(
        hidden,
        lax.all_gather(down_weight, "gy", axis=1, tiled=True),
        preferred_element_type=jnp.float32,
    )
    final_full, final_share = finish_sum(unit_partial, stream_full, feat_share)
    row_squares = jnp.sum(jnp.square(final_share.astype(jnp.float32)), axis=1)
    image_ids = group_index * IMG_GRP + jnp.arange(IMG_GRP, dtype=jnp.int32)
    member = segment_ids[:, None] == image_ids[None, :]
    image_sq = jnp.sum(jnp.where(member, row_squares[:, None], 0.0), axis=0)
    local_requests = lax.dynamic_slice_in_dim(image_requests, group_index * IMG_GRP, IMG_GRP)
    request_count = image_requests.shape[0] // 4
    owner = local_requests[:, None] == jnp.arange(request_count, dtype=jnp.int32)[None, :]
    request_part = jnp.sum(jnp.where(owner, image_sq[:, None], 0.0), axis=0)
    local_index = (merge_index - group_index * tok_rows).reshape(-1)
    joined = jnp.take(final_full, local_index, axis=0).reshape(
        merge_index.shape[0], 4 * final_full.shape[1]
    )
    logits = add_columns(joined, lax.all_gather(merge_weight, "gy", axis=0, tiled=True))
    local_top = jnp.max(logits)
    request_sq = lax.psum(request_part, ("gx", "gy"))
    top_logit = lax.pmax(local_top, ("gx", "gy"))
    return (logits.astype(jnp.bfloat16), jnp.sqrt(request_sq), top_logit)


def solution(mesh):
    in_specs = (
        P("gy", "gx"),
        P("gy"),
        P(),
        P("gy", None),
        P("gy", None, "gx"),
        P("gx", "gy"),
        P("gy", "gx"),
        P("gx", "gy"),
        P("gy", "gx"),
    )
    out_specs = (P("gy", "gx"), P(), P())
    return jax.shard_map(
        per_device, mesh=mesh, in_specs=in_specs, out_specs=out_specs, check_vma=False
    )
```

profile of v0, /device:TPU:0, one launch (start us, length us, event | category | flops | bytes accessed | tf_op | source)
XLA Modules:
  0.0 815.3 jit_solution(6109742581719975203)
XLA Ops:
  7.2 0.7 all-gather.7.cloned.1.call-update
  7.9 0.0 all-gather.9.cloned.1.call-start
  7.9 2.6 copy.29
  10.6 0.0 all-gather.11.cloned.1.call-start
  10.6 1.7 copy.32
  12.4 0.0 all-reduce.3.cloned.1.call-start
  12.4 1.0 broadcast_compare_fusion
  13.4 19.3 %all-gather.7.cloned.1.call-done = bf16[512,1664]{0,1:T(8,128)(2,1)} async-done(((bf16[512,416]{0,1:T(8,128)(2,1)}), bf16[512,1664]{0,1:T(8,128)(2,1)}) %all-gather.7.cloned.1.call-update) | async-done | bytes 1703952 | tf_op jit(solution)/shard_map/all_gather | solution.py:44
  32.7 2.7 copy.28
  35.4 0.6 convert_reduce_fusion.1
  36.1 104.4 %all-gather.9.cloned.1.call-done = bf16[1664,3,416]{2,1,0:T(4,128)(2,1)} async-done(((bf16[208,3,416]{2,1,0:T(4,128)(2,1)}), bf16[1664,3,416]{2,1,0:T(4,128)(2,1)}) %all-gather.9.cloned.1.call-update) | async-done | bytes 4153360 | tf_op jit(solution)/shard_map/all_gather | solution.py:48
  140.5 11.3 %copy.30 = bf16[1664,3,416]{0,2,1:T(8,128)(2,1)} copy(bf16[1664,3,416]{2,1,0:T(4,128)(2,1)} %all-gather.9.cloned.1.call-done) | data formatting | bytes 8306688 | tf_op jit(solution)/shard_map/all_gather | solution.py:48
  151.7 4.8 convolution_convert_fusion
  156.6 0.7 fusion.73
  157.3 2.1 fusion.109
  159.5 0.5 fusion.71
  160.0 26.7 %all-gather.11.cloned.1.call-done = bf16[416,1664]{0,1:T(8,128)(2,1)} async-done(((bf16[416,208]{0,1:T(8,128)(2,1)}), bf16[416,1664]{0,1:T(8,128)(2,1)}) %all-gather.11.cloned.1.call-update) | async-done | bytes 1384464 | tf_op jit(solution)/shard_map/all_gather | solution.py:60
  186.7 4.4 fusion.110
  191.1 0.0 all-gather.13.cloned.1.call-start
  191.1 0.5 all-gather.13.cloned.1.call-update
  191.7 0.0 all-gather.15.cloned.1.call-start
  191.7 0.5 all-gather.15.cloned.1.call-update
  192.3 0.2 all-reduce.5.cloned.1.call-start
  192.5 70.4 %all-reduce.3.cloned.1.call-done = f32[512,1664]{1,0:T(8,128)} async-done(((f32[512,1664]{1,0:T(8,128)}), f32[512,1664]{1,0:T(8,128)}) %all-reduce.3.cloned.1.call-update) | async-done | bytes 3407888 | tf_op jit(solution)/shard_map/psum | solution.py:24
  262.9 2.7 convert_reduce_fusion
  265.6 105.1 %all-gather.13.cloned.1.call-done = bf16[1664,2048]{1,0:T(8,128)(2,1)} async-done(((bf16[208,2048]{1,0:T(8,128)(2,1)}), bf16[1664,2048]{1,0:T(8,128)(2,1)}) %all-gather.13.cloned.1.call-update) | async-done | bytes 6815760 | tf_op jit(solution)/shard_map/all_gather | solution.py:65
  370.6 105.8 %all-gather.15.cloned.1.call-done = bf16[2048,1664]{0,1:T(8,128)(2,1)} async-done(((bf16[2048,208]{0,1:T(8,128)(2,1)}), bf16[2048,1664]{0,1:T(8,128)(2,1)}) %all-gather.15.cloned.1.call-update) | async-done | bytes 6815760 | tf_op jit(solution)/shard_map/all_gather | solution.py:69
  476.5 21.5 %fusion.20 = f32[512,1664]{1,0:T(8,128)} fusion(bf16[2048,1664]{0,1:T(8,128)(2,1)} %all-gather.15.cloned.1.call-done, bf16[1664,2048]{1,0:T(8,128)(2,1)} %all-gather.13.cloned.1.call-done, bf16[512,1664]{1,0:T(8,128)(2,1)S(1)} %get-tuple-element.7, f32[512]{0:T(512)S(1)} %get-tuple-element.13, f32[512]{0:T(512)S(1)} %get-tuple-element.12), kind=kOutput, calls=%fused_computation.42 | convolution fusion | flops 7050887168 | bytes 18747392 | tf_op jit(solution)/shard_map/dot_general | solution.py:67
  498.0 0.0 all-gather.17.cloned.1.call-start
  498.0 0.7 all-gather.17.cloned.1.call-update
  498.8 0.1 copy.33
  498.9 0.1 reshape.131
  499.0 0.1 copy.27
  499.1 0.1 dynamic_slice.6
  499.2 69.8 %all-reduce.5.cloned.1.call-done = f32[512,1664]{1,0:T(8,128)} async-done(((f32[512,1664]{1,0:T(8,128)}), f32[512,1664]{1,0:T(8,128)}) %all-reduce.5.cloned.1.call-update) | async-done | bytes 3407888 | tf_op jit(solution)/shard_map/psum | solution.py:24
  569.0 2.2 fusion.18
  571.2 0.4 multiply_reduce_fusion
  571.6 0.2 select_reduce_fusion
  571.8 0.1 select_reduce_fusion.1
  571.9 0.5 broadcast_in_dim.63
  572.4 1.3 copy.35
  573.8 42.4 %psum.23 = f32[8]{0:T(128)S(1)} all-reduce(f32[8]{0:T(128)S(1)} %select_reduce_fusion.1), channel_id=1, replica_groups=mesh['gx'=4,'gy'=8] {'gx','gy'}, use_global_device_ids=true, to_apply=%region_11.12 | all-reduce | flops 8 | bytes 64 | tf_op jit(solution)/shard_map/psum | solution.py:87
  616.2 2.3 gather_fusion
  618.5 1.2 gather.7
  619.7 0.5 sqrt.3
  620.2 141.2 %all-gather.17.cloned.1.call-done = bf16[6656,1024]{1,0:T(8,128)(2,1)} async-done(((bf16[832,1024]{1,0:T(8,128)(2,1)}), bf16[6656,1024]{1,0:T(8,128)(2,1)}) %all-gather.17.cloned.1.call-update) | async-done | bytes 13631504 | tf_op jit(solution)/shard_map/all_gather | solution.py:85
  761.5 8.4 %fusion.108 = (f32[]{:T(128)}, bf16[128,1024]{1,0:T(8,128)(2,1)}) fusion(bf16[6656,1024]{1,0:T(8,128)(2,1)} %all-gather.17.cloned.1.call-done, pred[128,6656]{1,0:T(8,128)(4,1)} %bitcast.26, bf16[128,6656]{1,0:T(8,128)(2,1)S(1)} %gather.7), kind=kOutput, calls=%fused_computation.138 | convolution fusion | flops 1745944576 | bytes 16449540 | tf_op jit(solution)/shard_map/dot_general | solution.py:19
  769.9 38.6 %pmax.7 = f32[]{:T(128)} all-reduce(f32[]{:T(128)} %get-tuple-element.10), channel_id=1, replica_groups=mesh['gx'=4,'gy'=8] {'gx','gy'}, use_global_device_ids=true, to_apply=%region_13.14 | all-reduce | flops 1 | bytes 8 | tf_op jit(solution)/shard_map/pmax | solution.py:88
  (17 shorter events, 0.2 us)
Async XLA Ops:
  7.2 25.5 %all-gather.7.cloned.1.call-start = ((), (), s32[]{:S(2)}) async-start(), calls=%async_computation | async-start | bytes 2129920 | tf_op jit(solution)/shard_map/all_gather | solution.py:44
  7.9 132.6 %all-gather.9.cloned.1.call-start = ((), (), s32[]{:S(2)}) async-start(), calls=%async_computation.1 | async-start | bytes 7667712 | tf_op jit(solution)/shard_map/all_gather | solution.py:48
  10.6 176.1 %all-gather.11.cloned.1.call-start = ((), (), s32[]{:S(2)}) async-start(), calls=%async_computation.2 | async-start | bytes 1916928 | tf_op jit(solution)/shard_map/all_gather | solution.py:60
  12.4 250.5 %all-reduce.3.cloned.1.call-start = ((), (), s32[]{:S(2)}) async-start(), calls=%async_computation.3 | async-start | bytes 6815744 | tf_op jit(solution)/shard_map/psum | solution.py:24
  191.1 179.6 %all-gather.13.cloned.1.call-start = ((), (), s32[]{:S(2)}) async-start(), calls=%async_computation.4 | async-start | bytes 7667712 | tf_op jit(solution)/shard_map/all_gather | solution.py:65
  191.7 284.8 %all-gather.15.cloned.1.call-start = ((), (), s32[]{:S(2)}) async-start(), calls=%async_computation.5 | async-start | bytes 7667712 | tf_op jit(solution)/shard_map/all_gather | solution.py:69
  192.3 376.7 %all-reduce.5.cloned.1.call-start = ((), (), s32[]{:S(2)}) async-start(), calls=%async_computation.6 | async-start | bytes 6815744 | tf_op jit(solution)/shard_map/psum | solution.py:24
  497.9 0.8 copy-start.1
  497.9 1.2 copy-start.2
  498.0 263.5 %all-gather.17.cloned.1.call-start = ((), (), s32[]{:S(2)}) async-start(), calls=%async_computation.7 | async-start | bytes 15335424 | tf_op jit(solution)/shard_map/all_gather | solution.py:85
  498.7 72.9 %copy-start = (s32[512]{0:T(512)S(1)}, s32[512]{0:T(512)}, u32[]{:S(2)}) copy-start(s32[512]{0:T(512)} %param.10) | copy-start | bytes 6148
Sparse Core Ops, SparseCore 0:
  9.6 23.0 all-gather.6
  34.9 105.5 all-gather.8
  143.2 43.4 all-gather.10
  191.2 71.6 all-reduce.2
  264.9 105.6 all-gather.12
  372.7 103.7 all-gather.14
  498.1 70.8 all-reduce.4
  571.2 190.2 all-gather.16
where the time goes:
time: 816 us; the launch traced here: 815 us
  waiting for transfers between devices  645 us (79%)
  blocking collectives  81.1 us (10%)
  matrix products  40.3 us (5%)
  local copies, waits for them, and re-layouts  24.7 us (3%)
  between operations  14.3 us (2%)
  other arithmetic  9.36 us (1%)
    all_gather x1, waiting for transfers between devices, per_device(): lax.all_gather(merge_weight, 'gy', axis=0, tiled=True)  141 us
    psum x2, waiting for transfers between devices, finish_sum(): summed = lax.psum(head_partial, 'gx')  140 us
    all_gather x1, waiting for transfers between devices, per_device(): lax.all_gather(down_weight, 'gy', axis=1, tiled=True)  106 us
    all_gather x1, waiting for transfers between devices, per_device(): lax.all_gather(up_weight, 'gy', axis=0, tiled=True)  105 us
    all_gather x1, waiting for transfers between devices, per_device(): lax.all_gather(qkv_weight, 'gy', axis=0, tiled=True)  104 us
    psum x1, blocking collectives, per_device(): request_sq = lax.psum(request_part, ('gx', 'gy'))  42.4 us
    pmax x1, blocking collectives, per_device(): top_logit = lax.pmax(local_top, ('gx', 'gy'))  38.6 us
    all_gather x1, waiting for transfers between devices, per_device(): lax.all_gather(out_weight, 'gy', axis=1, tiled=True)  26.7 us
  transfers between devices with their start and end apart: 8, of which 8 were waited for; matrix products, arithmetic and copies ran while one was open for 5% of the time, Pallas kernels for 0%

commit v1 on v0

--- a/solution.py
+++ b/solution.py
@@ -6,6 +6,17 @@
 
 HEAD = 104
 IMG_GRP = 4
+
+
+def collect(value, axis, dim):
+    ways = lax.axis_size(axis)
+    pieces = [value]
+    for far in range(1, ways):
+        pieces.append(
+            lax.ppermute(pieces[far - 1], axis, [(d, (d - 1) % ways) for d in range(ways)])
+        )
+    line = jnp.concatenate(pieces, axis=dim)
+    return jnp.roll(line, lax.axis_index(axis) * value.shape[dim], axis=dim)
 
 
 def layer_norm(values):
@@ -65,9 +76,7 @@
     hidden = add_columns(normed_two, lax.all_gather(up_weight, "gy", axis=0, tiled=True))
     hidden = jax.nn.gelu(hidden, approximate=False).astype(jnp.bfloat16)
     unit_partial = jnp.dot(
-        hidden,
-        lax.all_gather(down_weight, "gy", axis=1, tiled=True),
-        preferred_element_type=jnp.float32,
+        hidden, collect(down_weight, "gy", 1), preferred_element_type=jnp.float32
     )
     final_full, final_share = finish_sum(unit_partial, stream_full, feat_share)
     row_squares = jnp.sum(jnp.square(final_share.astype(jnp.float32)), axis=1)

time: 816 us -> 763 us (0.935)
  waiting for transfers between devices: 645 us -> 533 us
  starting transfers between devices: 0.5 us -> 33.9 us
  local copies, waits for them, and re-layouts: 24.7 us -> 49.2 us
    ppermute x0 -> x7, waiting for transfers between devices: none -> 131 us  [collect(): lax.ppermute(pieces[far - 1], axis, [(d, (d - 1) % ways) for d in range(w...]
    all_gather x1 -> x0, waiting for transfers between devices: 106 us -> none  [per_device(): lax.all_gather(down_weight, 'gy', axis=1, tiled=True)]
    all_gather x1, waiting for transfers between devices: 105 us -> 34.6 us  [per_device(): lax.all_gather(up_weight, 'gy', axis=0, tiled=True)]
    psum x2, waiting for transfers between devices: 140 us -> 74 us  [finish_sum(): summed = lax.psum(head_partial, 'gx')]
    ppermute x0 -> x7, starting transfers between devices: none -> 33.6 us  [collect(): lax.ppermute(pieces[far - 1], axis, [(d, (d - 1) % ways) for d in range(w...]
    unnamed x9 -> x38, local copies, waits for them, and re-layouts: 5.68 us -> 29.2 us
  transfers between devices with their start and end apart: 8 -> 14, of which waited for: 8 -> 13; matrix products, arithmetic and copies ran while one was open for 5% -> 8% of each run, Pallas kernels for 0% -> 0%
where the time goes in v1:
time: 763 us; the launch traced here: 762 us
  waiting for transfers between devices  533 us (70%)
  blocking collectives  81 us (11%)
  local copies, waits for them, and re-layouts  49.2 us (6%)
  matrix products  40.8 us (5%)
  starting transfers between devices  33.9 us (4%)
  between operations  14.3 us (2%)
  other arithmetic  9.36 us (1%)
    all_gather x1, waiting for transfers between devices, per_device(): lax.all_gather(merge_weight, 'gy', axis=0, tiled=True)  141 us
    ppermute x7, waiting for transfers between devices, collect(): lax.ppermute(pieces[far - 1], axis, [(d, (d - 1) % ways) for d in range(w...  131 us
    all_gather x1, waiting for transfers between devices, per_device(): lax.all_gather(qkv_weight, 'gy', axis=0, tiled=True)  104 us
    psum x2, waiting for transfers between devices, finish_sum(): summed = lax.psum(head_partial, 'gx')  74 us
    psum x1, blocking collectives, per_device(): request_sq = lax.psum(request_part, ('gx', 'gy'))  42.4 us
    pmax x1, blocking collectives, per_device(): top_logit = lax.pmax(local_top, ('gx', 'gy'))  38.6 us
    all_gather x1, waiting for transfers between devices, per_device(): lax.all_gather(up_weight, 'gy', axis=0, tiled=True)  34.6 us
    ppermute x7, starting transfers between devices, collect(): lax.ppermute(pieces[far - 1], axis, [(d, (d - 1) % ways) for d in range(w...  33.6 us
  transfers between devices with their start and end apart: 14, of which 13 were waited for; matrix products, arithmetic and copies ran while one was open for 8% of the time, Pallas kernels for 0%

profile of v1, /device:TPU:0, one launch (start us, length us, event | category | flops | bytes accessed | tf_op | source)
XLA Modules:
  0.0 762.0 jit_solution(6157236095673628723)
XLA Ops:
  7.9 2.6 copy.29
  10.6 1.7 copy.32
  12.5 1.0 broadcast_compare_fusion
  13.4 19.2 %all-gather.6.cloned.1.call-done = bf16[512,1664]{0,1:T(8,128)(2,1)} async-done(((bf16[512,416]{0,1:T(8,128)(2,1)}), bf16[512,1664]{0,1:T(8,128)(2,1)}) %all-gather.6.cloned.1.call-update) | async-done | bytes 1703952 | tf_op jit(solution)/shard_map/all_gather | solution.py:55
  32.7 2.7 copy.28
  36.1 104.4 %all-gather.8.cloned.1.call-done = bf16[1664,3,416]{2,1,0:T(4,128)(2,1)} async-done(((bf16[208,3,416]{2,1,0:T(4,128)(2,1)}), bf16[1664,3,416]{2,1,0:T(4,128)(2,1)}) %all-gather.8.cloned.1.call-update) | async-done | bytes 4153360 | tf_op jit(solution)/shard_map/all_gather | solution.py:59
  140.5 11.2 %copy.30 = bf16[1664,3,416]{0,2,1:T(8,128)(2,1)} copy(bf16[1664,3,416]{2,1,0:T(4,128)(2,1)} %all-gather.8.cloned.1.call-done) | data formatting | bytes 8306688 | tf_op jit(solution)/shard_map/all_gather | solution.py:59
  151.7 4.8 convolution_convert_fusion
  157.3 2.1 fusion.111
  159.9 26.8 %all-gather.10.cloned.1.call-done = bf16[416,1664]{0,1:T(8,128)(2,1)} async-done(((bf16[416,208]{0,1:T(8,128)(2,1)}), bf16[416,1664]{0,1:T(8,128)(2,1)}) %all-gather.10.cloned.1.call-update) | async-done | bytes 1384464 | tf_op jit(solution)/shard_map/all_gather | solution.py:71
  186.7 4.5 fusion.112
  191.9 2.3 collective-permute-start
  194.2 18.1 %collective-permute-done = bf16[2048,208]{0,1:T(8,128)(2,1)S(1)} collective-permute-done((bf16[2048,208]{0,1:T(8,128)(2,1)S(1)}, bf16[2048,208]{0,1:T(8,128)(2,1)S(1)}, u32[]{:S(2)}, u32[]{:S(2)}) %collective-permute-start) | collective-permute-done | bytes 852000 | tf_op jit(solution)/shard_map/ppermute | solution.py:16
  212.3 5.2 collective-permute-start.1
  217.5 17.2 %collective-permute-done.1 = bf16[2048,208]{0,1:T(8,128)(2,1)S(1)} collective-permute-done((bf16[2048,208]{0,1:T(8,128)(2,1)S(1)}, bf16[2048,208]{0,1:T(8,128)(2,1)S(1)}, u32[]{:S(2)}, u32[]{:S(2)}) %collective-permute-start.1) | collective-permute-done | bytes 852000 | tf_op jit(solution)/shard_map/ppermute | solution.py:16
  235.7 5.2 collective-permute-start.2
  240.9 16.3 %collective-permute-done.2 = bf16[2048,208]{0,1:T(8,128)(2,1)S(1)} collective-permute-done((bf16[2048,208]{0,1:T(8,128)(2,1)S(1)}, bf16[2048,208]{0,1:T(8,128)(2,1)S(1)}, u32[]{:S(2)}, u32[]{:S(2)}) %collective-permute-start.2) | collective-permute-done | bytes 852000 | tf_op jit(solution)/shard_map/ppermute | solution.py:16
  258.1 5.2 collective-permute-start.3
  263.3 25.4 %collective-permute-done.3 = bf16[2048,208]{0,1:T(8,128)(2,1)S(1)} collective-permute-done((bf16[2048,208]{0,1:T(8,128)(2,1)S(1)}, bf16[2048,208]{0,1:T(8,128)(2,1)S(1)}, u32[]{:S(2)}, u32[]{:S(2)}) %collective-permute-start.3) | collective-permute-done | bytes 852000 | tf_op jit(solution)/shard_map/ppermute | solution.py:16
  289.6 5.2 collective-permute-start.4
  294.9 31.9 %collective-permute-done.4 = bf16[2048,208]{0,1:T(8,128)(2,1)} collective-permute-done((bf16[2048,208]{0,1:T(8,128)(2,1)S(1)}, bf16[2048,208]{0,1:T(8,128)(2,1)}, u32[]{:S(2)}, u32[]{:S(2)}) %collective-permute-start.4) | collective-permute-done | bytes 852000 | tf_op jit(solution)/shard_map/ppermute | solution.py:16
  326.7 5.3 collective-permute-start.5
  333.0 1.0 constant_dynamic-update-slice_fusion.14
  334.0 2.1 constant_dynamic-update-slice_fusion.13
  336.2 9.8 %collective-permute-done.5 = bf16[2048,208]{0,1:T(8,128)(2,1)} collective-permute-done((bf16[2048,208]{0,1:T(8,128)(2,1)}, bf16[2048,208]{0,1:T(8,128)(2,1)}, u32[]{:S(2)}, u32[]{:S(2)}) %collective-permute-start.5) | collective-permute-done | bytes 852000 | tf_op jit(solution)/shard_map/ppermute | solution.py:16
  346.0 5.2 collective-permute-start.6
  352.2 1.0 constant_dynamic-update-slice_fusion.11
  353.2 2.2 constant_dynamic-update-slice_fusion.10
  355.4 2.2 constant_dynamic-update-slice_fusion.9
  357.6 12.5 %collective-permute-done.6 = bf16[2048,208]{0,1:T(8,128)(2,1)S(1)} collective-permute-done((bf16[2048,208]{0,1:T(8,128)(2,1)}, bf16[2048,208]{0,1:T(8,128)(2,1)S(1)}, u32[]{:S(2)}, u32[]{:S(2)}) %collective-permute-start.6) | collective-permute-done | bytes 852000 | tf_op jit(solution)/shard_map/ppermute | solution.py:16
  372.0 1.0 constant_dynamic-update-slice_fusion.6
  373.0 1.0 constant_dynamic-update-slice_fusion.5
  375.0 1.0 constant_dynamic-update-slice_fusion.3
  376.0 2.1 constant_dynamic-update-slice_fusion.2
  378.1 2.2 constant_dynamic-update-slice_fusion.1
  380.3 1.0 constant_dynamic-update-slice_fusion
  381.3 2.7 convert_reduce_fusion
  384.0 34.6 %all-gather.12.cloned.1.call-done = bf16[1664,2048]{1,0:T(8,128)(2,1)} async-done(((bf16[208,2048]{1,0:T(8,128)(2,1)}), bf16[1664,2048]{1,0:T(8,128)(2,1)}) %all-gather.12.cloned.1.call-update) | async-done | bytes 6815760 | tf_op jit(solution)/shard_map/all_gather | solution.py:76
  418.6 21.9 %fusion.1 = f32[512,1664]{1,0:T(8,128)} fusion(bf16[2048,3328]{0,1:T(8,128)(2,1)} %constant_dynamic-update-slice_fusion, s32[]{:T(128)S(6)} %select_n.56, bf16[1664,2048]{1,0:T(8,128)(2,1)} %all-gather.12.cloned.1.call-done, bf16[512,1664]{1,0:T(8,128)(2,1)S(1)} %get-tuple-element.7, f32[512]{0:T(512)S(1)} %get-tuple-element.13, f32[512]{0:T(512)S(1)} %get-tuple-element.12), kind=kOutput, calls=%fused_computation.2 | convolution fusion | flops 7050887168 | bytes 18747396 | tf_op jit(solution)/shard_map/dot_general | solution.py:78
  441.8 74.0 %all-reduce.5.cloned.1.call-done = f32[512,1664]{1,0:T(8,128)} async-done(((f32[512,1664]{1,0:T(8,128)}), f32[512,1664]{1,0:T(8,128)}) %all-reduce.5.cloned.1.call-update) | async-done | bytes 3407888 | tf_op jit(solution)/shard_map/psum | solution.py:35
  515.7 2.2 fusion.20
  519.2 1.3 copy.35
  520.5 42.4 %psum.23 = f32[8]{0:T(128)S(1)} all-reduce(f32[8]{0:T(128)S(1)} %select_reduce_fusion.1), channel_id=1, replica_groups=mesh['gx'=4,'gy'=8] {'gx','gy'}, use_global_device_ids=true, to_apply=%region_11.12 | all-reduce | flops 8 | bytes 64 | tf_op jit(solution)/shard_map/psum | solution.py:96
  562.9 2.3 gather_fusion
  565.3 1.2 gather.7
  567.0 141.2 %all-gather.14.cloned.1.call-done = bf16[6656,1024]{1,0:T(8,128)(2,1)} async-done(((bf16[832,1024]{1,0:T(8,128)(2,1)}), bf16[6656,1024]{1,0:T(8,128)(2,1)}) %all-gather.14.cloned.1.call-update) | async-done | bytes 13631504 | tf_op jit(solution)/shard_map/all_gather | solution.py:94
  708.2 8.4 %fusion.110 = (f32[]{:T(128)}, bf16[128,1024]{1,0:T(8,128)(2,1)}) fusion(bf16[6656,1024]{1,0:T(8,128)(2,1)} %all-gather.14.cloned.1.call-done, pred[128,6656]{1,0:T(8,128)(4,1)} %bitcast.25, bf16[128,6656]{1,0:T(8,128)(2,1)S(1)} %gather.7), kind=kOutput, calls=%fused_computation.156 | convolution fusion | flops 1745944576 | bytes 16449540 | tf_op jit(solution)/shard_map/dot_general | solution.py:30
  716.6 38.6 %pmax.7 = f32[]{:T(128)} all-reduce(f32[]{:T(128)} %get-tuple-element.10), channel_id=1, replica_groups=mesh['gx'=4,'gy'=8] {'gx','gy'}, use_global_device_ids=true, to_apply=%region_13.14 | all-reduce | flops 1 | bytes 8 | tf_op jit(solution)/shard_map/pmax | solution.py:97
  (58 shorter events, 13.9 us)
Async XLA Ops:
  7.2 25.5 %all-gather.6.cloned.1.call-start = ((), (), s32[]{:S(2)}) async-start(), calls=%async_computation | async-start | bytes 2129920 | tf_op jit(solution)/shard_map/all_gather | solution.py:55
  7.9 132.6 %all-gather.8.cloned.1.call-start = ((), (), s32[]{:S(2)}) async-start(), calls=%async_computation.1 | async-start | bytes 7667712 | tf_op jit(solution)/shard_map/all_gather | solution.py:59
  10.6 176.1 %all-gather.10.cloned.1.call-start = ((), (), s32[]{:S(2)}) async-start(), calls=%async_computation.2 | async-start | bytes 1916928 | tf_op jit(solution)/shard_map/all_gather | solution.py:71
  12.4 368.9 %all-reduce.3.cloned.1.call-start = ((), (), s32[]{:S(2)}) async-start(), calls=%async_computation.3 | async-start | bytes 6815744 | tf_op jit(solution)/shard_map/psum | solution.py:35
  186.7 5.2 copy-start
  191.2 227.4 %all-gather.12.cloned.1.call-start = ((), (), s32[]{:S(2)}) async-start(), calls=%async_computation.4 | async-start | bytes 7667712 | tf_op jit(solution)/shard_map/all_gather | solution.py:76
  191.8 323.9 %all-reduce.5.cloned.1.call-start = ((), (), s32[]{:S(2)}) async-start(), calls=%async_computation.5 | async-start | bytes 6815744 | tf_op jit(solution)/shard_map/psum | solution.py:35
  191.9 20.4 %collective-permute-start = (bf16[2048,208]{0,1:T(8,128)(2,1)S(1)}, bf16[2048,208]{0,1:T(8,128)(2,1)S(1)}, u32[]{:S(2)}, u32[]{:S(2)}) collective-permute-start(bf16[2048,208]{0,1:T(8,128)(2,1)S(1)} %copy-done), channel_id=1, source_target_pairs={{0,7},{1,0},{2,1},{3,2},{4,3},{5,4},{6,5},{7,6},{8,15},{9,8},{10,9... | collective-permute-start | bytes 2555912 | tf_op jit(solution)/shard_map/ppermute | solution.py:16
  212.3 22.4 %collective-permute-start.1 = (bf16[2048,208]{0,1:T(8,128)(2,1)S(1)}, bf16[2048,208]{0,1:T(8,128)(2,1)S(1)}, u32[]{:S(2)}, u32[]{:S(2)}) collective-permute-start(bf16[2048,208]{0,1:T(8,128)(2,1)S(1)} %collective-permute-done), channel_id=1, source_target_pairs={{0,7},{1,0},{2,1},{3,2},{4,3},{5,4},{6,5},{7,6},{8,15},{9,8},{10,9... | collective-permute-start | bytes 2555912 | tf_op jit(solution)/shard_map/ppermute | solution.py:16
  234.7 0.9 copy-start.1
  235.7 21.5 %collective-permute-start.2 = (bf16[2048,208]{0,1:T(8,128)(2,1)S(1)}, bf16[2048,208]{0,1:T(8,128)(2,1)S(1)}, u32[]{:S(2)}, u32[]{:S(2)}) collective-permute-start(bf16[2048,208]{0,1:T(8,128)(2,1)S(1)} %collective-permute-done.1), channel_id=1, source_target_pairs={{0,7},{1,0},{2,1},{3,2},{4,3},{5,4},{6,5},{7,6},{8,15},{9,8},{10,9... | collective-permute-start | bytes 2555912 | tf_op jit(solution)/shard_map/ppermute | solution.py:16
  257.2 0.9 copy-start.3
  258.1 30.6 %collective-permute-start.3 = (bf16[2048,208]{0,1:T(8,128)(2,1)S(1)}, bf16[2048,208]{0,1:T(8,128)(2,1)S(1)}, u32[]{:S(2)}, u32[]{:S(2)}) collective-permute-start(bf16[2048,208]{0,1:T(8,128)(2,1)S(1)} %collective-permute-done.2), channel_id=1, source_target_pairs={{0,7},{1,0},{2,1},{3,2},{4,3},{5,4},{6,5},{7,6},{8,15},{9,8},{10,9... | collective-permute-start | bytes 2555912 | tf_op jit(solution)/shard_map/ppermute | solution.py:16
  288.7 0.9 copy-start.5
  289.6 37.1 %collective-permute-start.4 = (bf16[2048,208]{0,1:T(8,128)(2,1)S(1)}, bf16[2048,208]{0,1:T(8,128)(2,1)}, u32[]{:S(2)}, u32[]{:S(2)}) collective-permute-start(bf16[2048,208]{0,1:T(8,128)(2,1)S(1)} %collective-permute-done.3), channel_id=1, source_target_pairs={{0,7},{1,0},{2,1},{3,2},{4,3},{5,4},{6,5},{7,6},{8,15},{9,8},{10,9... | collective-permute-start | bytes 2555912 | tf_op jit(solution)/shard_map/ppermute | solution.py:16
  326.7 19.3 %collective-permute-start.5 = (bf16[2048,208]{0,1:T(8,128)(2,1)}, bf16[2048,208]{0,1:T(8,128)(2,1)}, u32[]{:S(2)}, u32[]{:S(2)}) collective-permute-start(bf16[2048,208]{0,1:T(8,128)(2,1)} %collective-permute-done.4), channel_id=1, source_target_pairs={{0,7},{1,0},{2,1},{3,2},{4,3},{5,4},{6,5},{7,6},{8,15},{9,8},{10,9... | collective-permute-start | bytes 2555912 | tf_op jit(solution)/shard_map/ppermute | solution.py:16
  332.1 19.2 %copy-start.4 = (bf16[2048,208]{0,1:T(8,128)(2,1)S(1)}, bf16[2048,208]{0,1:T(8,128)(2,1)}, u32[]{:S(2)}) copy-start(bf16[2048,208]{0,1:T(8,128)(2,1)} %copy-done.3) | copy-start | bytes 2555908
  332.1 20.1 %copy-start.6 = (bf16[2048,208]{0,1:T(8,128)(2,1)S(1)}, bf16[2048,208]{0,1:T(8,128)(2,1)}, u32[]{:S(2)}) copy-start(bf16[2048,208]{0,1:T(8,128)(2,1)} %copy-done.5) | copy-start | bytes 2555908
  346.0 24.0 %collective-permute-start.6 = (bf16[2048,208]{0,1:T(8,128)(2,1)}, bf16[2048,208]{0,1:T(8,128)(2,1)S(1)}, u32[]{:S(2)}, u32[]{:S(2)}) collective-permute-start(bf16[2048,208]{0,1:T(8,128)(2,1)} %collective-permute-done.5), channel_id=1, source_target_pairs={{0,7},{1,0},{2,1},{3,2},{4,3},{5,4},{6,5},{7,6},{8,15},{9,8},{10,9... | collective-permute-start | bytes 2555912 | tf_op jit(solution)/shard_map/ppermute | solution.py:16
  353.2 19.8 %copy-start.2 = (bf16[2048,208]{0,1:T(8,128)(2,1)S(1)}, bf16[2048,208]{0,1:T(8,128)(2,1)}, u32[]{:S(2)}) copy-start(bf16[2048,208]{0,1:T(8,128)(2,1)} %copy-done.1) | copy-start | bytes 2555908
  440.5 0.8 copy-start.8
  440.5 1.2 copy-start.9
  440.5 267.7 %all-gather.14.cloned.1.call-start = ((), (), s32[]{:S(2)}) async-start(), calls=%async_computation.6 | async-start | bytes 15335424 | tf_op jit(solution)/shard_map/all_gather | solution.py:94
  441.3 77.1 %copy-start.7 = (s32[512]{0:T(512)S(1)}, s32[512]{0:T(512)}, u32[]{:S(2)}) copy-start(s32[512]{0:T(512)} %param.10) | copy-start | bytes 6148
Sparse Core Ops, SparseCore 0:
  9.6 23.0 all-gather.5
  34.9 105.5 all-gather.7
  143.2 43.4 all-gather.9
  191.4 71.6 all-reduce.2
  265.1 153.5 all-gather.11
  440.6 75.0 all-reduce.4
  517.9 190.2 all-gather.13
